TPU v7x, 256 devices: a whole 4x4x8 slice. The times are simulated.
256 devices in a mesh: dp: 32 (over z, y), ep: 8 (over x, core).
Axes of the slice: x: 4, y: 4, z: 8, core: 2. Of those that a mesh axis runs over, the one named last changes fastest.
Arguments:
- states: bfloat16 [2048, 16, 128, 128], P(('dp', 'ep')), may hold values from -4 to 4
- query_rows: bfloat16 [2048, 4, 1024], P(('dp', 'ep')), may hold values from -6 to 6
- key_rows: bfloat16 [2048, 4, 1024], P(('dp', 'ep')), may hold values from -6 to 6
- value_rows: bfloat16 [2048, 4, 2048], P(('dp', 'ep')), may hold values from -6 to 6
- gate_rows: bfloat16 [2048, 4, 2048], P(('dp', 'ep')), may hold values from -6 to 6
- beta_logit: bfloat16 [2048, 4, 16], P(('dp', 'ep')), may hold values from -6 to 6
- decay_logit: bfloat16 [2048, 4, 16], P(('dp', 'ep')), may hold values from -8 to 8
- residual: bfloat16 [2048, 4, 2048], P(('dp', 'ep')), may hold values from -6 to 6
- route_ids: int32 [2048, 4, 10], P(('dp', 'ep')), may hold values from 0 to 255, all different within a row; in each aligned block of 32 rows (0 to 31, 32 to 63, ..., all dimensions but the last counted through in order) at most 3 rows name the same one
- route_prob: float32 [2048, 4, 10], P(('dp', 'ep')), may hold values from 0.05 to 1
- out_weight: bfloat16 [2048, 2048], P(None, 'ep'), may hold values from -0.125 to 0.125
- core_gain: float32 [128], replicated, may hold values from 0.1 to 1.9
- moe_gain: float32 [2048], replicated, may hold values from 0.1 to 1.9
- gate_up: bfloat16 [256, 2048, 512], P(('dp', 'ep')), may hold values from -0.125 to 0.125
- down_weight: bfloat16 [256, 256, 2048], P(('dp', 'ep')), may hold values from -0.375 to 0.375
- new_home: int32 [2048], P(('dp', 'ep')), may hold values from 0 to 2047, as said below
Outputs:
- mixed_out: bfloat16 [2048, 4, 2048], P(('dp', 'ep'))
- moved_out: bfloat16 [2048, 16, 128, 128], P(('dp', 'ep'))
Inputs may be any that keep to these rules, and one draw needn't show every extreme that they name: `route_ids`: each row names 10 different experts; among the 32 rows of one device (its requests, each with its 4 tokens) no expert is named more than 3 times, a bound that some block reaches. `new_home`: A permutation of the request positions; a request stays among the 8 devices of its dp index, and every device hands exactly 1 of its requests to each device of that group, itself included.
All inputs are finite; a program needn't handle non-finite values.
Results may differ from a plain program's by a relative error of at most 0.01.
Values may be sent and summed in bfloat16 or wider, within the bound.
A program may use at most 128 MiB of HBM per device.

v0:
```python
import jax
import jax.numpy as jnp
from jax import lax
from jax.sharding import PartitionSpec as P

epsilon = 1e-06


def unit_rows(values):
    return values * lax.rsqrt(jnp.sum(values * values, -1, keepdims=True) + epsilon)


def delta_block(
    state_in, query_rows, key_rows, value_rows, gate_rows, beta_logit, decay_logit, core_gain
):
    batch_size = state_in.shape[0]
    head_count = decay_logit.shape[-1]
    head_width = state_in.shape[-1]
    key_heads = query_rows.shape[-1] // head_width
    repeats = head_count // key_heads
    memory_state = state_in.astype(jnp.float32)
    outputs = []
    for position in range(query_rows.shape[1]):
        queries = unit_rows(
            query_rows[:, position].astype(jnp.float32).reshape(batch_size, key_heads, head_width)
        )
        queries = jnp.repeat(queries, repeats, axis=1) * head_width ** (-0.5)
        key_units = unit_rows(
            key_rows[:, position].astype(jnp.float32).reshape(batch_size, key_heads, head_width)
        )
        key_units = jnp.repeat(key_units, repeats, axis=1)
        values = (
            value_rows[:, position].astype(jnp.float32).reshape(batch_size, head_count, head_width)
        )
        decays = jax.nn.sigmoid(decay_logit[:, position].astype(jnp.float32))
        strength = jax.nn.sigmoid(beta_logit[:, position].astype(jnp.float32))
        memory_state = memory_state * decays[:, :, None, None]
        memory = jnp.einsum(
            "bhkv,bhk->bhv", memory_state, key_units, precision=lax.Precision.HIGHEST
        )
        update = (values - memory) * strength[:, :, None]
        memory_state = memory_state + key_units[:, :, :, None] * update[:, :, None, :]
        reading = jnp.einsum(
            "bhkv,bhk->bhv", memory_state, queries, precision=lax.Precision.HIGHEST
        )
        scaled = reading * lax.rsqrt(jnp.mean(reading * reading, -1, keepdims=True) + epsilon)
        gate_vals = (
            gate_rows[:, position].astype(jnp.float32).reshape(batch_size, head_count, head_width)
        )
        gated_out = scaled * core_gain * jax.nn.silu(gate_vals)
        outputs.append(gated_out.reshape(batch_size, head_count * head_width).astype(jnp.bfloat16))
    return (memory_state.astype(jnp.bfloat16), jnp.stack(outputs, axis=1))


def rms_scale(values, gain):
    return values * lax.rsqrt(jnp.mean(values * values, -1, keepdims=True) + epsilon) * gain


def expert_apply(chosen_rows, gate_up, down_weight):
    hidden_units = down_weight.shape[0]
    joined = jnp.dot(chosen_rows, gate_up, preferred_element_type=jnp.float32)
    active = (jax.nn.silu(joined[:, :hidden_units]) * joined[:, hidden_units:]).astype(jnp.bfloat16)
    return jnp.dot(active, down_weight, preferred_element_type=jnp.float32).astype(jnp.bfloat16)


def pack(values, positions, lane_count):
    zeroed = jnp.zeros(values.shape, values.dtype)
    placed = zeroed.at[positions].set(values)
    return placed.reshape((lane_count, values.shape[0] // lane_count) + values.shape[1:])


def unpack(values):
    return values.reshape((values.shape[0] * values.shape[1],) + values.shape[2:])


def shards(
    states,
    query_rows,
    key_rows,
    value_rows,
    gate_rows,
    beta_logit,
    decay_logit,
    residual,
    route_ids,
    route_prob,
    out_weight,
    core_gain,
    moe_gain,
    gate_up,
    down_weight,
    new_home,
):
    req_count = states.shape[0]
    step_count = query_rows.shape[1]
    model_width = residual.shape[-1]
    ep_size = lax.axis_size("ep")
    dp_size = lax.axis_size("dp")
    target = new_home // req_count % ep_size
    new_place = new_home % req_count
    order_ids = jnp.arange(req_count, dtype=jnp.int32)
    earlier = (target[:, None] == target[None, :]) & (order_ids[None, :] < order_ids[:, None])
    lane_rank = jnp.sum(earlier.astype(jnp.int32), axis=1)
    lane_cap = req_count // ep_size
    buffer_index = target * lane_cap + lane_rank
    fresh_states, core_out = delta_block(
        states, query_rows, key_rows, value_rows, gate_rows, beta_logit, decay_logit, core_gain
    )
    received = (
        lax.all_to_all(
            pack(fresh_states, buffer_index, ep_size), "ep", split_axis=0, concat_axis=0, tiled=True
        ),
        lax.all_to_all(
            pack(new_place, buffer_index, ep_size), "ep", split_axis=0, concat_axis=0, tiled=True
        ),
    )
    moved_out = jnp.zeros_like(states).at[unpack(received[1])].set(unpack(received[0]), mode="drop")
    token_count = req_count * step_count
    core_flat = core_out.reshape(token_count, core_out.shape[-1])
    columns = jnp.dot(
        lax.all_gather(core_flat, "ep", axis=0, tiled=True),
        out_weight,
        preferred_element_type=jnp.float32,
    ).astype(jnp.bfloat16)
    attention = lax.all_to_all(columns, "ep", split_axis=0, concat_axis=1, tiled=True)
    hidden = (
        residual.reshape(token_count, model_width).astype(jnp.float32)
        + attention.astype(jnp.float32)
    ).astype(jnp.bfloat16)
    normed = rms_scale(hidden.astype(jnp.float32), moe_gain).astype(jnp.bfloat16)
    top_count = route_ids.shape[-1]
    experts = dp_size * ep_size
    capacity = (token_count * top_count + experts - 1) // experts + 1
    flat_ids = route_ids.reshape(-1)
    onehot = (flat_ids[:, None] == jnp.arange(experts, dtype=jnp.int32)[None, :]).astype(jnp.int32)
    route_rank = jnp.sum(jnp.cumsum(onehot, axis=0) * onehot, axis=1) - 1
    slot_index = flat_ids * capacity + route_rank
    outgoing = (
        jnp.zeros((experts * capacity, model_width), jnp.bfloat16)
        .at[slot_index]
        .set(jnp.repeat(normed, top_count, axis=0))
    )
    arrived = lax.all_to_all(
        lax.all_to_all(
            outgoing.reshape(dp_size, ep_size, capacity, model_width),
            "dp",
            split_axis=0,
            concat_axis=0,
            tiled=True,
        ),
        "ep",
        split_axis=1,
        concat_axis=1,
        tiled=True,
    )
    result = expert_apply(arrived.reshape(-1, model_width), gate_up[0], down_weight[0]).reshape(
        dp_size, ep_size, capacity, model_width
    )
    returned = lax.all_to_all(
        lax.all_to_all(result, "dp", split_axis=0, concat_axis=0, tiled=True),
        "ep",
        split_axis=1,
        concat_axis=1,
        tiled=True,
    )
    routed = returned.reshape(experts * capacity, model_width)[slot_index]
    weights = route_prob.reshape(token_count, top_count)
    weights = weights / jnp.sum(weights, -1, keepdims=True)
    combined = jnp.sum(
        routed.reshape(token_count, top_count, model_width).astype(jnp.float32)
        * weights[:, :, None],
        axis=1,
    )
    mixed_out = (
        (hidden.astype(jnp.float32) + combined)
        .astype(jnp.bfloat16)
        .reshape(req_count, step_count, model_width)
    )
    return (mixed_out, moved_out)


def solution(mesh):
    placed = (
        P(("dp", "ep"), None, None, None),
        P(("dp", "ep"), None, None),
        P(("dp", "ep"), None, None),
        P(("dp", "ep"), None, None),
        P(("dp", "ep"), None, None),
        P(("dp", "ep"), None, None),
        P(("dp", "ep"), None, None),
        P(("dp", "ep"), None, None),
        P(("dp", "ep"), None, None),
        P(("dp", "ep"), None, None),
        P(None, "ep"),
        P(),
        P(),
        P(("dp", "ep"), None, None),
        P(("dp", "ep"), None, None),
        P(("dp", "ep")),
    )
    return jax.shard_map(
        shards,
        mesh=mesh,
        in_specs=placed,
        out_specs=(P(("dp", "ep"), None, None), P(("dp", "ep"), None, None, None)),
        check_vma=False,
    )
```

profile of v0, /device:TPU:24, one launch (start us, length us, event | category | flops | bytes accessed | tf_op | source)
XLA Modules:
  0.0 571.1 jit_solution(461292190551067246)
XLA Ops:
  14.3 9.7 %fusion = f32[8,16,1,128]{3,2,1,0:T(1,128)S(1)} fusion(f32[8,16,128,1]{2,3,1,0:T(1,128)S(1)} %bitcast.152, bf16[8,16,128,128]{3,2,1,0:T(8,128)(2,1)} %param.16, f32[8,16]{1,0:T(8,128)S(1)} %get-tuple-element.37), kind=kOutput, calls=%fused_computation.10 | convolution fusion | flops 29360128 | bytes 4325888 | tf_op jit(solution)/shard_map/bhkv,bhk->bhv/dot_general | solution.py:38
  24.1 8.3 %fusion.2 = f32[8,16,1,128]{3,2,1,0:T(1,128)S(1)} fusion(f32[8,16,128,1]{2,3,1,0:T(1,128)S(1)} %bitcast.196, bf16[8,16,128,128]{3,2,1,0:T(8,128)(2,1)S(1)} %copy-done.1, f32[8,16,128]{2,1,0:T(8,128)S(1)} %subtract_multiply_fusion.3, f32[8,16,128]{2,1,0:T(8,128)S(1)} %bitcast.153, f32[8,16]{1,0:T(8,128)S(1)} %get-tuple-element.37), kind=kOutput, calls=%fused_computation.12 | convolution fusion | flops 33554432 | bytes 4456960 | tf_op jit(solution)/shard_map/bhkv,bhk->bhv/dot_general | solution.py:43
  32.6 9.0 %fusion.3 = f32[8,16,1,128]{3,2,1,0:T(1,128)S(1)} fusion(f32[8,16,128,1]{2,3,1,0:T(1,128)S(1)} %bitcast.161, bf16[8,16,128,128]{3,2,1,0:T(8,128)(2,1)S(1)} %copy-done.1, f32[8,16]{1,0:T(8,128)S(1)} %get-tuple-element.36, f32[8,16,128]{2,1,0:T(8,128)S(1)} %subtract_multiply_fusion.3, f32[8,16,128]{2,1,0:T(8,128)S(1)} %bitcast.154, ...), kind=kOutput, calls=%fused_computation.13 | convolution fusion | flops 35651584 | bytes 4457472 | tf_op jit(solution)/shard_map/bhkv,bhk->bhv/dot_general | solution.py:38
  41.7 11.6 %fusion.11 = f32[8,16,1,128]{3,2,1,0:T(1,128)S(1)} fusion(f32[8,16,128,1]{2,3,1,0:T(1,128)S(1)} %bitcast.197, bf16[8,16,128,128]{3,2,1,0:T(8,128)(2,1)S(1)} %copy-done.1, f32[8,16,128]{2,1,0:T(8,128)S(1)} %subtract_multiply_fusion.2, f32[8,16,128]{2,1,0:T(8,128)S(1)} %bitcast.162, f32[8,16]{1,0:T(8,128)S(1)} %get-tuple-element.36, ...), kind=kOutput, calls=%fused_computation.20 | convolution fusion | flops 39845888 | bytes 4588544 | tf_op jit(solution)/shard_map/bhkv,bhk->bhv/dot_general | solution.py:43
  53.4 11.7 %fusion.7 = f32[8,16,1,128]{3,2,1,0:T(1,128)S(1)} fusion(f32[8,16,128,1]{2,3,1,0:T(1,128)S(1)} %bitcast.168, bf16[8,16,128,128]{3,2,1,0:T(8,128)(2,1)S(1)} %copy-done.1, f32[8,16]{1,0:T(8,128)S(1)} %get-tuple-element.35, f32[8,16,128]{2,1,0:T(8,128)S(1)} %subtract_multiply_fusion.2, f32[8,16,128]{2,1,0:T(8,128)S(1)} %bitcast.163, ...), kind=kOutput, calls=%fused_computation.16 | convolution fusion | flops 41943040 | bytes 4589056 | tf_op jit(solution)/shard_map/bhkv,bhk->bhv/dot_general | solution.py:38
  65.2 15.5 %fusion.43 = f32[8,16,1,128]{3,2,1,0:T(1,128)S(1)} fusion(f32[8,16,128,1]{2,3,1,0:T(1,128)S(1)} %bitcast.198, bf16[8,16,128,128]{3,2,1,0:T(8,128)(2,1)S(1)} %copy-done.1, f32[8,16,128]{2,1,0:T(8,128)S(1)} %subtract_multiply_fusion.1, f32[8,16,128]{2,1,0:T(8,128)S(1)} %bitcast.169, f32[8,16]{1,0:T(8,128)S(1)} %get-tuple-element.35, ...), kind=kOutput, calls=%fused_computation.56 | convolution fusion | flops 46137344 | bytes 4720128 | tf_op jit(solution)/shard_map/bhkv,bhk->bhv/dot_general | solution.py:43
  80.9 15.6 %fusion.5 = f32[8,16,1,128]{3,2,1,0:T(1,128)S(1)} fusion(f32[8,16,128,1]{2,3,1,0:T(1,128)S(1)} %bitcast.173, f32[8,16]{1,0:T(8,128)S(1)} %get-tuple-element.34, bf16[8,16,128,128]{3,2,1,0:T(8,128)(2,1)S(1)} %copy-done.1, f32[8,16,128]{2,1,0:T(8,128)S(1)} %subtract_multiply_fusion.1, f32[8,16,128]{2,1,0:T(8,128)S(1)} %bitcast.170, ...), kind=kOutput, calls=%fused_computation.14 | convolution fusion | flops 48234496 | bytes 4720640 | tf_op jit(solution)/shard_map/bhkv,bhk->bhv/dot_general | solution.py:38
  96.8 21.1 %fusion.10 = f32[8,16,1,128]{3,2,1,0:T(1,128)S(1)} fusion(f32[8,16,128,1]{2,3,1,0:T(1,128)S(1)} %bitcast.199, f32[8,16,128]{2,1,0:T(8,128)S(1)} %subtract_multiply_fusion, f32[8,16,128]{2,1,0:T(8,128)S(1)} %bitcast.174, f32[8,16]{1,0:T(8,128)S(1)} %get-tuple-element.34, bf16[8,16,128,128]{3,2,1,0:T(8,128)(2,1)S(1)} %copy-done.1, ...), kind=kOutput, calls=%fused_computation.19 | convolution fusion | flops 52428800 | bytes 4851712 | tf_op jit(solution)/shard_map/bhkv,bhk->bhv/dot_general | solution.py:43
  120.4 27.7 %all-gather.2.cloned.1.call-done = bf16[256,2048]{1,0:T(8,128)(2,1)} async-done(((bf16[32,2048]{1,0:T(8,128)(2,1)}), bf16[256,2048]{1,0:T(8,128)(2,1)}) %all-gather.2.cloned.1.call-update) | async-done | bytes 1048592 | tf_op jit(solution)/shard_map/all_gather | solution.py:121
  172.3 9.1 %reshape.504 = bf16[32,8,3,2048]{3,2,1,0:T(4,128)(2,1)} reshape(bf16[768,2048]{1,0:T(8,128)(2,1)} %scatter_custom_fusion) | data formatting | bytes 6291456 | tf_op jit(solution)/shard_map/reshape | solution.py:145
  186.9 82.7 %all_to_all.50 = bf16[32,8,3,2048]{3,1,2,0:T(8,128)(2,1)S(1)} all-to-all(bf16[32,8,3,2048]{3,1,2,0:T(8,128)(2,1)S(1)} %copy.104), channel_id=1, replica_groups=mesh['dp'=32,'ep'=8] {'dp'}, dimensions={0} | all-to-all | bytes 6291456 | tf_op jit(solution)/shard_map/all_to_all | solution.py:144
  279.1 36.9 %all-to-all-done.2 = bf16[32,8,3,2048]{3,0,2,1:T(8,128)(2,1)} async-done(((bf16[32,8,3,2048]{3,0,2,1:T(8,128)(2,1)}), bf16[32,8,3,2048]{3,0,2,1:T(8,128)(2,1)}, u32[]{:S(2)}, u32[]{:S(2)}) %all-to-all-start.2) | async-done | bytes 3145760 | tf_op jit(solution)/shard_map/all_to_all | solution.py:143
  319.6 6.6 %copy.106 = bf16[32,8,3,2048]{3,2,1,0:T(4,128)(2,1)} copy(bf16[32,8,3,2048]{3,0,2,1:T(8,128)(2,1)} %all-to-all-done.2) | data formatting | bytes 6291456 | tf_op jit(solution)/shard_map/all_to_all | solution.py:143
  326.2 8.8 %reshape.505 = bf16[768,2048]{1,0:T(8,128)(2,1)} reshape(bf16[32,8,3,2048]{3,2,1,0:T(4,128)(2,1)} %copy.106) | data formatting | bytes 6291456 | tf_op jit(solution)/shard_map/reshape | solution.py:156
  341.5 9.1 %reshape.506 = bf16[32,8,3,2048]{3,2,1,0:T(4,128)(2,1)} reshape(bf16[768,2048]{1,0:T(8,128)(2,1)} %convolution_convert_fusion) | data formatting | bytes 6291456 | tf_op jit(solution)/shard_map/reshape | solution.py:156
  350.6 7.2 %copy.107 = bf16[32,8,3,2048]{3,1,2,0:T(8,128)(2,1)} copy(bf16[32,8,3,2048]{3,2,1,0:T(4,128)(2,1)} %reshape.506) | data formatting | bytes 6291456 | tf_op jit(solution)/shard_map/reshape | solution.py:156
  363.7 13.3 %fusion.9 = bf16[8,16,128,128]{3,2,1,0:T(8,128)(2,1)} fusion(f32[8,16,128]{2,1,0:T(8,128)S(1)} %copy-done.13, f32[8,16,128]{2,1,0:T(8,128)S(1)} %bitcast.175, f32[8,16]{1,0:T(8,128)S(1)} %get-tuple-element.34, f32[8,16,128]{2,1,0:T(8,128)S(1)} %copy-done.11, f32[8,16,128]{2,1,0:T(8,128)S(1)} %bitcast.172, f32[8,16]{1,0:T(8,128)S(1)} %get-tuple-element.35, ...), kind=kLoop, calls=%fused_computation.18 | loop fusion | flops 29360128 | bytes 8914944 | tf_op jit(solution)/shard_map/convert_element_type | solution.py:52
  380.0 10.9 %scatter_fusion = bf16[8,16,128,128]{3,2,1,0:T(8,128)(2,1)} fusion(bf16[8,16,128,128]{3,2,1,0:T(8,128)(2,1)} %broadcast.332.clone, s32[8]{0:T(128)S(1)} %compare_select_fusion.2, bf16[8,16,128,128]{3,2,1,0:T(8,128)(2,1)} %fusion.9), kind=kCustom, calls=%fused_computation.3 | custom fusion | bytes 12582944 | tf_op jit(solution)/shard_map/scatter | solution.py:68
  390.9 46.9 %all-to-all-done.3 = bf16[32,8,3,2048]{3,1,2,0:T(8,128)(2,1)} async-done(((bf16[32,8,3,2048]{3,1,2,0:T(8,128)(2,1)}), bf16[32,8,3,2048]{3,1,2,0:T(8,128)(2,1)}, u32[]{:S(2)}, u32[]{:S(2)}) %all-to-all-start.3) | async-done | bytes 3145760 | tf_op jit(solution)/shard_map/all_to_all | solution.py:160
  447.9 44.3 %all-to-all-done.6 = bf16[8,1,16,128,128]{4,3,2,1,0:T(8,128)(2,1)} async-done(((bf16[8,1,16,128,128]{4,3,2,1,0:T(8,128)(2,1)}), bf16[8,1,16,128,128]{4,3,2,1,0:T(8,128)(2,1)}, u32[]{:S(2)}, u32[]{:S(2)}) %all-to-all-start.6) | async-done | bytes 4194336 | tf_op jit(solution)/shard_map/all_to_all | solution.py:110
  500.8 10.9 %scatter_fusion.1 = bf16[8,16,128,128]{3,2,1,0:T(8,128)(2,1)} fusion(bf16[8,16,128,128]{3,2,1,0:T(8,128)(2,1)} %broadcast.332, s32[8]{0:T(128)S(1)} %fusion.54, bf16[8,16,128,128]{3,2,1,0:T(8,128)(2,1)} %bitcast.77), kind=kCustom, calls=%fused_computation.4 | custom fusion | bytes 12582944 | tf_op jit(solution)/shard_map/scatter | solution.py:117
  511.7 23.4 %all-to-all-done.4 = bf16[32,8,3,2048]{3,0,2,1:T(8,128)(2,1)} async-done(((bf16[32,8,3,2048]{3,0,2,1:T(8,128)(2,1)}), bf16[32,8,3,2048]{3,0,2,1:T(8,128)(2,1)}, u32[]{:S(2)}, u32[]{:S(2)}) %all-to-all-start.4) | async-done | bytes 3145760 | tf_op jit(solution)/shard_map/all_to_all | solution.py:159
  541.6 8.8 %reshape.507 = bf16[768,2048]{1,0:T(8,128)(2,1)} reshape(bf16[32,8,3,2048]{3,2,1,0:T(4,128)(2,1)} %copy.109) | data formatting | bytes 6291456 | tf_op jit(solution)/shard_map/reshape | solution.py:166
  550.4 6.8 %gather_fusion = bf16[320,2048]{1,0:T(8,128)(2,1)S(1)} fusion(bf16[768,2048]{1,0:T(8,128)(2,1)} %reshape.507, s32[1024]{0:T(1024)} %pad_clamp_fusion), kind=kCustom, calls=%fused_computation | custom fusion | bytes 2622720 | tf_op jit(solution)/shard_map/gather | solution.py:166
  (177 shorter events, 99.9 us)
Async XLA Ops:
  7.2 327.9 %copy-start = (bf16[1,2048,512]{2,1,0:T(8,128)(2,1)S(1)}, bf16[1,2048,512]{2,1,0:T(8,128)(2,1)}, u32[]{:S(2)}) copy-start(bf16[1,2048,512]{2,1,0:T(8,128)(2,1)} %param.29) | copy-start | bytes 6291460
  7.2 140.9 %all-gather.2.cloned.1.call-start = ((), (), s32[]{:S(2)}) async-start(), calls=%async_computation.7 | async-start | bytes 1179648 | tf_op jit(solution)/shard_map/all_gather | solution.py:121
  9.0 15.1 %copy-start.1 = (bf16[8,16,128,128]{3,2,1,0:T(8,128)(2,1)S(1)}, bf16[8,16,128,128]{3,2,1,0:T(8,128)(2,1)}, u32[]{:S(2)}) copy-start(bf16[8,16,128,128]{3,2,1,0:T(8,128)(2,1)} %param.16) | copy-start | bytes 12582916
  14.3 82.4 %copy-start.14 = (f32[8,8,2,128]{3,2,1,0:T(2,128)}, f32[8,8,2,128]{3,2,1,0:T(2,128)S(1)}, u32[]{:S(2)}) copy-start(f32[8,8,2,128]{3,2,1,0:T(2,128)S(1)} %broadcast_in_dim.22) | copy-start | bytes 196612
  24.1 72.6 %copy-start.6 = (f32[8,16,128]{2,1,0:T(8,128)}, f32[8,16,128]{2,1,0:T(8,128)S(1)}, u32[]{:S(2)}) copy-start(f32[8,16,128]{2,1,0:T(8,128)S(1)} %subtract_multiply_fusion.3) | copy-start | bytes 196612
  32.6 64.1 %copy-start.16 = (f32[8,8,2,128]{3,2,1,0:T(2,128)}, f32[8,8,2,128]{3,2,1,0:T(2,128)S(1)}, u32[]{:S(2)}) copy-start(f32[8,8,2,128]{3,2,1,0:T(2,128)S(1)} %broadcast_in_dim.24) | copy-start | bytes 196612
  41.6 55.1 %copy-start.8 = (f32[8,16,128]{2,1,0:T(8,128)}, f32[8,16,128]{2,1,0:T(8,128)S(1)}, u32[]{:S(2)}) copy-start(f32[8,16,128]{2,1,0:T(8,128)S(1)} %subtract_multiply_fusion.2) | copy-start | bytes 196612
  53.4 43.3 %copy-start.18 = (f32[8,8,2,128]{3,2,1,0:T(2,128)}, f32[8,8,2,128]{3,2,1,0:T(2,128)S(1)}, u32[]{:S(2)}) copy-start(f32[8,8,2,128]{3,2,1,0:T(2,128)S(1)} %broadcast_in_dim.26) | copy-start | bytes 196612
  65.2 31.5 %copy-start.10 = (f32[8,16,128]{2,1,0:T(8,128)}, f32[8,16,128]{2,1,0:T(8,128)S(1)}, u32[]{:S(2)}) copy-start(f32[8,16,128]{2,1,0:T(8,128)S(1)} %subtract_multiply_fusion.1) | copy-start | bytes 196612
  80.9 15.8 %copy-start.20 = (f32[8,8,2,128]{3,2,1,0:T(2,128)}, f32[8,8,2,128]{3,2,1,0:T(2,128)S(1)}, u32[]{:S(2)}) copy-start(f32[8,8,2,128]{3,2,1,0:T(2,128)S(1)} %broadcast_in_dim.28) | copy-start | bytes 196612
  96.6 21.3 %copy-start.12 = (f32[8,16,128]{2,1,0:T(8,128)}, f32[8,16,128]{2,1,0:T(8,128)S(1)}, u32[]{:S(2)}) copy-start(f32[8,16,128]{2,1,0:T(8,128)S(1)} %subtract_multiply_fusion) | copy-start | bytes 196612
  96.7 21.3 %copy-start.5 = (bf16[8,4,2048]{2,1,0:T(4,128)(2,1)S(1)}, bf16[8,4,2048]{2,1,0:T(4,128)(2,1)}, u32[]{:S(2)}) copy-start(bf16[8,4,2048]{2,1,0:T(4,128)(2,1)} %param.20) | copy-start | bytes 393220
  96.8 21.5 %copy-start.25 = (f32[128]{0:T(128)S(1)}, f32[128]{0:T(128)}, u32[]{:S(2)}) copy-start(f32[128]{0:T(128)} %param.27) | copy-start | bytes 1540
  96.8 22.6 %copy-start.22 = (s32[8,4,10]{2,1,0:T(4,128)S(1)}, s32[8,4,10]{2,1,0:T(4,128)}, u32[]{:S(2)}) copy-start(s32[8,4,10]{2,1,0:T(4,128)} %param.24) | copy-start | bytes 3844
  118.2 36.2 %copy-start.4 = (bf16[8,4,2048]{2,1,0:T(4,128)(2,1)S(1)}, bf16[8,4,2048]{2,1,0:T(4,128)(2,1)}, u32[]{:S(2)}) copy-start(bf16[8,4,2048]{2,1,0:T(4,128)(2,1)} %param.23) | copy-start | bytes 393220
  150.7 9.6 %all-to-all-start = ((bf16[8,32,256]{2,1,0:T(8,128)(2,1)}), bf16[8,32,256]{2,1,0:T(8,128)(2,1)S(1)}, u32[]{:S(2)}, u32[]{:S(2)}) async-start(bf16[8,32,256]{2,1,0:T(8,128)(2,1)} %bitcast.64), calls=%async_computation | async-start | bytes 262144 | tf_op jit(solution)/shard_map/all_to_all | solution.py:125
  160.7 11.7 %copy-start.2 = (f32[8,4,2048]{2,1,0:T(4,128)}, f32[8,4,2048]{2,1,0:T(4,128)S(1)}, u32[]{:S(2)}) copy-start(f32[8,4,2048]{2,1,0:T(4,128)S(1)} %reshape.543) | copy-start | bytes 786436
  273.1 43.0 %all-to-all-start.2 = ((bf16[32,8,3,2048]{3,0,2,1:T(8,128)(2,1)}), bf16[32,8,3,2048]{3,0,2,1:T(8,128)(2,1)}, u32[]{:S(2)}, u32[]{:S(2)}) async-start(bf16[32,8,3,2048]{3,0,2,1:T(8,128)(2,1)} %copy.105), calls=%async_computation.2 | async-start | bytes 6291456 | tf_op jit(solution)/shard_map/all_to_all | solution.py:143
  316.1 41.8 %all-to-all-start.5 = ((s32[8,1,1]{2,1,0:T(1,128)}), s32[8,1,1]{2,1,0:T(1,128)S(1)}, u32[]{:S(2)}, u32[]{:S(2)}) async-start(s32[8,1,1]{2,1,0:T(1,128)} %copy.110), calls=%async_computation.5 | async-start | bytes 8192 | tf_op jit(solution)/shard_map/all_to_all | solution.py:113
  357.9 79.9 %all-to-all-start.3 = ((bf16[32,8,3,2048]{3,1,2,0:T(8,128)(2,1)}), bf16[32,8,3,2048]{3,1,2,0:T(8,128)(2,1)}, u32[]{:S(2)}, u32[]{:S(2)}) async-start(bf16[32,8,3,2048]{3,1,2,0:T(8,128)(2,1)} %copy.107), calls=%async_computation.3 | async-start | bytes 6291456 | tf_op jit(solution)/shard_map/all_to_all | solution.py:160
  437.7 54.5 %all-to-all-start.6 = ((bf16[8,1,16,128,128]{4,3,2,1,0:T(8,128)(2,1)}), bf16[8,1,16,128,128]{4,3,2,1,0:T(8,128)(2,1)}, u32[]{:S(2)}, u32[]{:S(2)}) async-start(bf16[8,1,16,128,128]{4,3,2,1,0:T(8,128)(2,1)} %bitcast.132), calls=%async_computation.6 | async-start | bytes 8388608 | tf_op jit(solution)/shard_map/all_to_all | solution.py:110
  447.9 48.8 %copy-start.23 = (f32[8,4,10]{2,1,0:T(4,128)S(1)}, f32[8,4,10]{2,1,0:T(4,128)}, u32[]{:S(2)}) copy-start(f32[8,4,10]{2,1,0:T(4,128)} %param.25) | copy-start | bytes 3844
  447.9 49.0 %copy-start.24 = (s32[320]{0:T(512)S(1)}, s32[320]{0:T(512)}, u32[]{:S(2)}) copy-start(s32[320]{0:T(512)} %fusion.52) | copy-start | bytes 3844
  492.2 42.9 %all-to-all-start.4 = ((bf16[32,8,3,2048]{3,0,2,1:T(8,128)(2,1)}), bf16[32,8,3,2048]{3,0,2,1:T(8,128)(2,1)}, u32[]{:S(2)}, u32[]{:S(2)}) async-start(bf16[32,8,3,2048]{3,0,2,1:T(8,128)(2,1)} %copy.108), calls=%async_computation.4 | async-start | bytes 6291456 | tf_op jit(solution)/shard_map/all_to_all | solution.py:159
  (11 other events, 58.8 us)
Sparse Core Ops, SparseCore 0:
  119.5 28.5 all-gather.1
where the time goes:
time: 577 us; the launch traced here: 571 us
  waiting for transfers between devices  185 us (32%)
  local copies, waits for them, and re-layouts  123 us (21%)
  matrix products  112 us (19%)
  blocking collectives  82.7 us (14%)
  other arithmetic  27.5 us (5%)
  starting transfers between devices  26.7 us (5%)
  between operations  15.4 us (3%)
    all_to_all x1, blocking collectives, shards(): lax.all_to_all(outgoing.reshape(dp_size, ep_size, capacity, model_width),...  82.7 us
    dot_general x4, matrix products, delta_block(): jnp.einsum('bhkv,bhk->bhv', memory_state, queries, precision=lax.Precisio...  56.5 us
    all_to_all x1, waiting for transfers between devices, shards(): lax.all_to_all(result, 'dp', split_axis=0, concat_axis=0, tiled=True)  46.9 us
    dot_general x4, matrix products, delta_block(): jnp.einsum('bhkv,bhk->bhv', memory_state, key_units, precision=lax.Precis...  45.9 us
    all_to_all x1, waiting for transfers between devices, shards(): lax.all_to_all(pack(fresh_states, buffer_index, ep_size), 'ep', split_axi...  44.3 us
    all_to_all x1, waiting for transfers between devices, shards(): lax.all_to_all(lax.all_to_all(outgoing.reshape(dp_size, ep_size, capacity...  36.9 us
    all_gather x1, waiting for transfers between devices, shards(): lax.all_gather(core_flat, 'ep', axis=0, tiled=True)  27.7 us
    all_to_all x1, waiting for transfers between devices, shards(): lax.all_to_all(lax.all_to_all(result, 'dp', split_axis=0, concat_axis=0,...  23.4 us
  transfers between devices with their start and end apart: 7, of which 6 were waited for; matrix products, arithmetic and copies ran while one was open for 16% of the time, Pallas kernels for 0%

commit v1 on v0

--- a/solution.py
+++ b/solution.py
@@ -4,6 +4,13 @@
 from jax.sharding import PartitionSpec as P
 
 epsilon = 1e-06
+
+
+def create_forms_by_axis(along_axis, patch):
+    z = jnp.concatenate(
+        lax.all_to_all(jnp.stack(lax.axis_size(along_axis) * [patch]), along_axis, 0, 0), axis=0
+    )
+    return z
 
 
 def unit_rows(values):
@@ -118,9 +125,7 @@
     token_count = req_count * step_count
     core_flat = core_out.reshape(token_count, core_out.shape[-1])
     columns = jnp.dot(
-        lax.all_gather(core_flat, "ep", axis=0, tiled=True),
-        out_weight,
-        preferred_element_type=jnp.float32,
+        create_forms_by_axis("ep", core_flat), out_weight, preferred_element_type=jnp.float32
     ).astype(jnp.bfloat16)
     attention = lax.all_to_all(columns, "ep", split_axis=0, concat_axis=1, tiled=True)
     hidden = (

time: 577 us -> 557 us (0.965)
  waiting for transfers between devices: 185 us -> 170 us
  between operations: 15.4 us -> 1.99 us
    all_gather x1 -> x0, waiting for transfers between devices: 27.7 us -> none  [shards(): lax.all_gather(core_flat, 'ep', axis=0, tiled=True)]
    all_to_all x0 -> x1, waiting for transfers between devices: none -> 13.1 us  [create_forms_by_axis(): lax.all_to_all(jnp.stack(lax.axis_size(along_axis) * [patch]), along_axis...]
where the time goes in v1:
time: 557 us; the launch traced here: 551 us
  waiting for transfers between devices  170 us (31%)
  local copies, waits for them, and re-layouts  124 us (22%)
  matrix products  111 us (20%)
  blocking collectives  84.1 us (15%)
  starting transfers between devices  31.1 us (6%)
  other arithmetic  28.5 us (5%)
    all_to_all x1, blocking collectives, shards(): lax.all_to_all(outgoing.reshape(dp_size, ep_size, capacity, model_width),...  84.1 us
    dot_general x4, matrix products, delta_block(): jnp.einsum('bhkv,bhk->bhv', memory_state, queries, precision=lax.Precisio...  56.5 us
    all_to_all x1, waiting for transfers between devices, shards(): lax.all_to_all(result, 'dp', split_axis=0, concat_axis=0, tiled=True)  46.9 us
    dot_general x4, matrix products, delta_block(): jnp.einsum('bhkv,bhk->bhv', memory_state, key_units, precision=lax.Precis...  45.9 us
    all_to_all x1, waiting for transfers between devices, shards(): lax.all_to_all(pack(fresh_states, buffer_index, ep_size), 'ep', split_axi...  44.3 us
    all_to_all x1, waiting for transfers between devices, shards(): lax.all_to_all(lax.all_to_all(outgoing.reshape(dp_size, ep_size, capacity...  36.9 us
    all_to_all x1, waiting for transfers between devices, shards(): lax.all_to_all(lax.all_to_all(result, 'dp', split_axis=0, concat_axis=0,...  23.4 us
    reshape x2, local copies, waits for them, and re-layouts, shards(): expert_apply(arrived.reshape(-1, model_width), gate_up[0], down_weight[0])  16.3 us
  transfers between devices with their start and end apart: 7, of which 6 were waited for; matrix products, arithmetic and copies ran while one was open for 16% of the time, Pallas kernels for 0%

profile of v1, /device:TPU:24, one launch (start us, length us, event | category | flops | bytes accessed | tf_op | source)
XLA Modules:
  0.0 550.8 jit_solution(10348469416959453216)
XLA Ops:
  7.7 9.7 %fusion = f32[8,16,1,128]{3,2,1,0:T(1,128)S(1)} fusion(f32[8,16,128,1]{2,3,1,0:T(1,128)S(1)} %bitcast.154, bf16[8,16,128,128]{3,2,1,0:T(8,128)(2,1)} %param.16, f32[8,16]{1,0:T(8,128)S(1)} %get-tuple-element.37), kind=kOutput, calls=%fused_computation.10 | convolution fusion | flops 29360128 | bytes 4325888 | tf_op jit(solution)/shard_map/bhkv,bhk->bhv/dot_general | solution.py:45
  17.6 8.3 %fusion.2 = f32[8,16,1,128]{3,2,1,0:T(1,128)S(1)} fusion(f32[8,16,128,1]{2,3,1,0:T(1,128)S(1)} %bitcast.198, bf16[8,16,128,128]{3,2,1,0:T(8,128)(2,1)S(1)} %copy-done.1, f32[8,16,128]{2,1,0:T(8,128)S(1)} %subtract_multiply_fusion.3, f32[8,16,128]{2,1,0:T(8,128)S(1)} %bitcast.155, f32[8,16]{1,0:T(8,128)S(1)} %get-tuple-element.37), kind=kOutput, calls=%fused_computation.12 | convolution fusion | flops 33554432 | bytes 4456960 | tf_op jit(solution)/shard_map/bhkv,bhk->bhv/dot_general | solution.py:50
  26.0 9.0 %fusion.3 = f32[8,16,1,128]{3,2,1,0:T(1,128)S(1)} fusion(f32[8,16,128,1]{2,3,1,0:T(1,128)S(1)} %bitcast.163, bf16[8,16,128,128]{3,2,1,0:T(8,128)(2,1)S(1)} %copy-done.1, f32[8,16]{1,0:T(8,128)S(1)} %get-tuple-element.36, f32[8,16,128]{2,1,0:T(8,128)S(1)} %subtract_multiply_fusion.3, f32[8,16,128]{2,1,0:T(8,128)S(1)} %bitcast.156, ...), kind=kOutput, calls=%fused_computation.13 | convolution fusion | flops 35651584 | bytes 4457472 | tf_op jit(solution)/shard_map/bhkv,bhk->bhv/dot_general | solution.py:45
  35.1 11.6 %fusion.11 = f32[8,16,1,128]{3,2,1,0:T(1,128)S(1)} fusion(f32[8,16,128,1]{2,3,1,0:T(1,128)S(1)} %bitcast.199, bf16[8,16,128,128]{3,2,1,0:T(8,128)(2,1)S(1)} %copy-done.1, f32[8,16,128]{2,1,0:T(8,128)S(1)} %subtract_multiply_fusion.2, f32[8,16,128]{2,1,0:T(8,128)S(1)} %bitcast.164, f32[8,16]{1,0:T(8,128)S(1)} %get-tuple-element.36, ...), kind=kOutput, calls=%fused_computation.20 | convolution fusion | flops 39845888 | bytes 4588544 | tf_op jit(solution)/shard_map/bhkv,bhk->bhv/dot_general | solution.py:50
  46.9 11.7 %fusion.7 = f32[8,16,1,128]{3,2,1,0:T(1,128)S(1)} fusion(f32[8,16,128,1]{2,3,1,0:T(1,128)S(1)} %bitcast.170, bf16[8,16,128,128]{3,2,1,0:T(8,128)(2,1)S(1)} %copy-done.1, f32[8,16]{1,0:T(8,128)S(1)} %get-tuple-element.35, f32[8,16,128]{2,1,0:T(8,128)S(1)} %subtract_multiply_fusion.2, f32[8,16,128]{2,1,0:T(8,128)S(1)} %bitcast.165, ...), kind=kOutput, calls=%fused_computation.16 | convolution fusion | flops 41943040 | bytes 4589056 | tf_op jit(solution)/shard_map/bhkv,bhk->bhv/dot_general | solution.py:45
  58.7 15.5 %fusion.43 = f32[8,16,1,128]{3,2,1,0:T(1,128)S(1)} fusion(f32[8,16,128,1]{2,3,1,0:T(1,128)S(1)} %bitcast.200, bf16[8,16,128,128]{3,2,1,0:T(8,128)(2,1)S(1)} %copy-done.1, f32[8,16,128]{2,1,0:T(8,128)S(1)} %subtract_multiply_fusion.1, f32[8,16,128]{2,1,0:T(8,128)S(1)} %bitcast.171, f32[8,16]{1,0:T(8,128)S(1)} %get-tuple-element.35, ...), kind=kOutput, calls=%fused_computation.56 | convolution fusion | flops 46137344 | bytes 4720128 | tf_op jit(solution)/shard_map/bhkv,bhk->bhv/dot_general | solution.py:50
  74.3 15.6 %fusion.5 = f32[8,16,1,128]{3,2,1,0:T(1,128)S(1)} fusion(f32[8,16,128,1]{2,3,1,0:T(1,128)S(1)} %bitcast.175, f32[8,16]{1,0:T(8,128)S(1)} %get-tuple-element.34, bf16[8,16,128,128]{3,2,1,0:T(8,128)(2,1)S(1)} %copy-done.1, f32[8,16,128]{2,1,0:T(8,128)S(1)} %subtract_multiply_fusion.1, f32[8,16,128]{2,1,0:T(8,128)S(1)} %bitcast.172, ...), kind=kOutput, calls=%fused_computation.14 | convolution fusion | flops 48234496 | bytes 4720640 | tf_op jit(solution)/shard_map/bhkv,bhk->bhv/dot_general | solution.py:45
  90.2 21.1 %fusion.10 = f32[8,16,1,128]{3,2,1,0:T(1,128)S(1)} fusion(f32[8,16,128,1]{2,3,1,0:T(1,128)S(1)} %bitcast.201, f32[8,16,128]{2,1,0:T(8,128)S(1)} %subtract_multiply_fusion, f32[8,16,128]{2,1,0:T(8,128)S(1)} %bitcast.176, f32[8,16]{1,0:T(8,128)S(1)} %get-tuple-element.34, bf16[8,16,128,128]{3,2,1,0:T(8,128)(2,1)S(1)} %copy-done.1, ...), kind=kOutput, calls=%fused_computation.19 | convolution fusion | flops 52428800 | bytes 4851712 | tf_op jit(solution)/shard_map/bhkv,bhk->bhv/dot_general | solution.py:50
  120.5 13.1 %all-to-all-done = bf16[8,32,2048]{2,1,0:T(8,128)(2,1)S(1)} async-done(((bf16[8,32,2048]{2,1,0:T(8,128)(2,1)}), bf16[8,32,2048]{2,1,0:T(8,128)(2,1)S(1)}, u32[]{:S(2)}, u32[]{:S(2)}) %all-to-all-start) | async-done | bytes 1048608 | tf_op jit(solution)/shard_map/all_to_all | solution.py:11
  157.5 9.1 %reshape.506 = bf16[32,8,3,2048]{3,2,1,0:T(4,128)(2,1)} reshape(bf16[768,2048]{1,0:T(8,128)(2,1)} %scatter_custom_fusion) | data formatting | bytes 6291456 | tf_op jit(solution)/shard_map/reshape | solution.py:150
  172.1 84.1 %all_to_all.55 = bf16[32,8,3,2048]{3,1,2,0:T(8,128)(2,1)S(1)} all-to-all(bf16[32,8,3,2048]{3,1,2,0:T(8,128)(2,1)S(1)} %copy.104), channel_id=1, replica_groups=mesh['dp'=32,'ep'=8] {'dp'}, dimensions={0} | all-to-all | bytes 6291456 | tf_op jit(solution)/shard_map/all_to_all | solution.py:149
  265.7 36.9 %all-to-all-done.3 = bf16[32,8,3,2048]{3,0,2,1:T(8,128)(2,1)} async-done(((bf16[32,8,3,2048]{3,0,2,1:T(8,128)(2,1)}), bf16[32,8,3,2048]{3,0,2,1:T(8,128)(2,1)}, u32[]{:S(2)}, u32[]{:S(2)}) %all-to-all-start.3) | async-done | bytes 3145760 | tf_op jit(solution)/shard_map/all_to_all | solution.py:148
  306.1 6.6 %copy.106 = bf16[32,8,3,2048]{3,2,1,0:T(4,128)(2,1)} copy(bf16[32,8,3,2048]{3,0,2,1:T(8,128)(2,1)} %all-to-all-done.3) | data formatting | bytes 6291456 | tf_op jit(solution)/shard_map/all_to_all | solution.py:148
  312.7 8.8 %reshape.507 = bf16[768,2048]{1,0:T(8,128)(2,1)} reshape(bf16[32,8,3,2048]{3,2,1,0:T(4,128)(2,1)} %copy.106) | data formatting | bytes 6291456 | tf_op jit(solution)/shard_map/reshape | solution.py:161
  328.0 9.1 %reshape.508 = bf16[32,8,3,2048]{3,2,1,0:T(4,128)(2,1)} reshape(bf16[768,2048]{1,0:T(8,128)(2,1)} %convolution_convert_fusion) | data formatting | bytes 6291456 | tf_op jit(solution)/shard_map/reshape | solution.py:161
  337.1 7.2 %copy.107 = bf16[32,8,3,2048]{3,1,2,0:T(8,128)(2,1)} copy(bf16[32,8,3,2048]{3,2,1,0:T(4,128)(2,1)} %reshape.508) | data formatting | bytes 6291456 | tf_op jit(solution)/shard_map/reshape | solution.py:161
  350.3 13.3 %fusion.9 = bf16[8,16,128,128]{3,2,1,0:T(8,128)(2,1)} fusion(f32[8,16,128]{2,1,0:T(8,128)S(1)} %copy-done.14, f32[8,16,128]{2,1,0:T(8,128)S(1)} %bitcast.177, f32[8,16]{1,0:T(8,128)S(1)} %get-tuple-element.34, f32[8,16,128]{2,1,0:T(8,128)S(1)} %copy-done.12, f32[8,16,128]{2,1,0:T(8,128)S(1)} %bitcast.174, f32[8,16]{1,0:T(8,128)S(1)} %get-tuple-element.35, ...), kind=kLoop, calls=%fused_computation.18 | loop fusion | flops 29360128 | bytes 8914944 | tf_op jit(solution)/shard_map/convert_element_type | solution.py:59
  366.6 10.9 %scatter_fusion = bf16[8,16,128,128]{3,2,1,0:T(8,128)(2,1)} fusion(bf16[8,16,128,128]{3,2,1,0:T(8,128)(2,1)} %broadcast.333.clone, s32[8]{0:T(128)S(1)} %compare_select_fusion.2, bf16[8,16,128,128]{3,2,1,0:T(8,128)(2,1)} %fusion.9), kind=kCustom, calls=%fused_computation.3 | custom fusion | bytes 12582944 | tf_op jit(solution)/shard_map/scatter | solution.py:75
  377.4 46.9 %all-to-all-done.4 = bf16[32,8,3,2048]{3,1,2,0:T(8,128)(2,1)} async-done(((bf16[32,8,3,2048]{3,1,2,0:T(8,128)(2,1)}), bf16[32,8,3,2048]{3,1,2,0:T(8,128)(2,1)}, u32[]{:S(2)}, u32[]{:S(2)}) %all-to-all-start.4) | async-done | bytes 3145760 | tf_op jit(solution)/shard_map/all_to_all | solution.py:165
  434.4 44.3 %all-to-all-done.7 = bf16[8,1,16,128,128]{4,3,2,1,0:T(8,128)(2,1)} async-done(((bf16[8,1,16,128,128]{4,3,2,1,0:T(8,128)(2,1)}), bf16[8,1,16,128,128]{4,3,2,1,0:T(8,128)(2,1)}, u32[]{:S(2)}, u32[]{:S(2)}) %all-to-all-start.7) | async-done | bytes 4194336 | tf_op jit(solution)/shard_map/all_to_all | solution.py:117
  487.4 10.9 %scatter_fusion.1 = bf16[8,16,128,128]{3,2,1,0:T(8,128)(2,1)} fusion(bf16[8,16,128,128]{3,2,1,0:T(8,128)(2,1)} %broadcast.333, s32[8]{0:T(128)S(1)} %fusion.54, bf16[8,16,128,128]{3,2,1,0:T(8,128)(2,1)} %bitcast.78), kind=kCustom, calls=%fused_computation.4 | custom fusion | bytes 12582944 | tf_op jit(solution)/shard_map/scatter | solution.py:124
  498.2 23.4 %all-to-all-done.5 = bf16[32,8,3,2048]{3,0,2,1:T(8,128)(2,1)} async-done(((bf16[32,8,3,2048]{3,0,2,1:T(8,128)(2,1)}), bf16[32,8,3,2048]{3,0,2,1:T(8,128)(2,1)}, u32[]{:S(2)}, u32[]{:S(2)}) %all-to-all-start.5) | async-done | bytes 3145760 | tf_op jit(solution)/shard_map/all_to_all | solution.py:164
  528.2 8.8 %reshape.509 = bf16[768,2048]{1,0:T(8,128)(2,1)} reshape(bf16[32,8,3,2048]{3,2,1,0:T(4,128)(2,1)} %copy.109) | data formatting | bytes 6291456 | tf_op jit(solution)/shard_map/reshape | solution.py:171
  537.0 6.8 %gather_fusion = bf16[320,2048]{1,0:T(8,128)(2,1)S(1)} fusion(bf16[768,2048]{1,0:T(8,128)(2,1)} %reshape.509, s32[1024]{0:T(1024)} %pad_clamp_fusion), kind=kCustom, calls=%fused_computation | custom fusion | bytes 2622720 | tf_op jit(solution)/shard_map/gather | solution.py:171
  (179 shorter events, 106.2 us)
Async XLA Ops:
  0.6 320.9 %copy-start = (bf16[1,2048,512]{2,1,0:T(8,128)(2,1)S(1)}, bf16[1,2048,512]{2,1,0:T(8,128)(2,1)}, u32[]{:S(2)}) copy-start(bf16[1,2048,512]{2,1,0:T(8,128)(2,1)} %param.29) | copy-start | bytes 6291460
  2.4 15.1 %copy-start.1 = (bf16[8,16,128,128]{3,2,1,0:T(8,128)(2,1)S(1)}, bf16[8,16,128,128]{3,2,1,0:T(8,128)(2,1)}, u32[]{:S(2)}) copy-start(bf16[8,16,128,128]{3,2,1,0:T(8,128)(2,1)} %param.16) | copy-start | bytes 12582916
  7.7 82.4 %copy-start.15 = (f32[8,8,2,128]{3,2,1,0:T(2,128)}, f32[8,8,2,128]{3,2,1,0:T(2,128)S(1)}, u32[]{:S(2)}) copy-start(f32[8,8,2,128]{3,2,1,0:T(2,128)S(1)} %broadcast_in_dim.22) | copy-start | bytes 196612
  17.5 72.6 %copy-start.7 = (f32[8,16,128]{2,1,0:T(8,128)}, f32[8,16,128]{2,1,0:T(8,128)S(1)}, u32[]{:S(2)}) copy-start(f32[8,16,128]{2,1,0:T(8,128)S(1)} %subtract_multiply_fusion.3) | copy-start | bytes 196612
  26.0 64.1 %copy-start.17 = (f32[8,8,2,128]{3,2,1,0:T(2,128)}, f32[8,8,2,128]{3,2,1,0:T(2,128)S(1)}, u32[]{:S(2)}) copy-start(f32[8,8,2,128]{3,2,1,0:T(2,128)S(1)} %broadcast_in_dim.24) | copy-start | bytes 196612
  35.1 55.1 %copy-start.9 = (f32[8,16,128]{2,1,0:T(8,128)}, f32[8,16,128]{2,1,0:T(8,128)S(1)}, u32[]{:S(2)}) copy-start(f32[8,16,128]{2,1,0:T(8,128)S(1)} %subtract_multiply_fusion.2) | copy-start | bytes 196612
  46.9 43.3 %copy-start.19 = (f32[8,8,2,128]{3,2,1,0:T(2,128)}, f32[8,8,2,128]{3,2,1,0:T(2,128)S(1)}, u32[]{:S(2)}) copy-start(f32[8,8,2,128]{3,2,1,0:T(2,128)S(1)} %broadcast_in_dim.26) | copy-start | bytes 196612
  58.6 31.5 %copy-start.11 = (f32[8,16,128]{2,1,0:T(8,128)}, f32[8,16,128]{2,1,0:T(8,128)S(1)}, u32[]{:S(2)}) copy-start(f32[8,16,128]{2,1,0:T(8,128)S(1)} %subtract_multiply_fusion.1) | copy-start | bytes 196612
  74.3 15.8 %copy-start.21 = (f32[8,8,2,128]{3,2,1,0:T(2,128)}, f32[8,8,2,128]{3,2,1,0:T(2,128)S(1)}, u32[]{:S(2)}) copy-start(f32[8,8,2,128]{3,2,1,0:T(2,128)S(1)} %broadcast_in_dim.28) | copy-start | bytes 196612
  90.1 21.3 %copy-start.13 = (f32[8,16,128]{2,1,0:T(8,128)}, f32[8,16,128]{2,1,0:T(8,128)S(1)}, u32[]{:S(2)}) copy-start(f32[8,16,128]{2,1,0:T(8,128)S(1)} %subtract_multiply_fusion) | copy-start | bytes 196612
  90.2 21.3 %copy-start.6 = (bf16[8,4,2048]{2,1,0:T(4,128)(2,1)S(1)}, bf16[8,4,2048]{2,1,0:T(4,128)(2,1)}, u32[]{:S(2)}) copy-start(bf16[8,4,2048]{2,1,0:T(4,128)(2,1)} %param.20) | copy-start | bytes 393220
  90.2 21.5 %copy-start.26 = (f32[128]{0:T(128)S(1)}, f32[128]{0:T(128)}, u32[]{:S(2)}) copy-start(f32[128]{0:T(128)} %param.27) | copy-start | bytes 1540
  111.3 6.3 %copy-start.23 = (s32[8,4,10]{2,1,0:T(4,128)S(1)}, s32[8,4,10]{2,1,0:T(4,128)}, u32[]{:S(2)}) copy-start(s32[8,4,10]{2,1,0:T(4,128)} %param.24) | copy-start | bytes 3844
  113.2 26.4 %copy-start.5 = (bf16[8,4,2048]{2,1,0:T(4,128)(2,1)S(1)}, bf16[8,4,2048]{2,1,0:T(4,128)(2,1)}, u32[]{:S(2)}) copy-start(bf16[8,4,2048]{2,1,0:T(4,128)(2,1)} %param.23) | copy-start | bytes 393220
  113.2 20.4 %all-to-all-start = ((bf16[8,32,2048]{2,1,0:T(8,128)(2,1)}), bf16[8,32,2048]{2,1,0:T(8,128)(2,1)S(1)}, u32[]{:S(2)}, u32[]{:S(2)}) async-start(bf16[8,32,2048]{2,1,0:T(8,128)(2,1)} %stack.5), calls=%async_computation | async-start | bytes 2097152 | tf_op jit(solution)/shard_map/all_to_all | solution.py:11
  135.9 9.6 %all-to-all-start.1 = ((bf16[8,32,256]{2,1,0:T(8,128)(2,1)}), bf16[8,32,256]{2,1,0:T(8,128)(2,1)S(1)}, u32[]{:S(2)}, u32[]{:S(2)}) async-start(bf16[8,32,256]{2,1,0:T(8,128)(2,1)} %bitcast.65), calls=%async_computation.1 | async-start | bytes 262144 | tf_op jit(solution)/shard_map/all_to_all | solution.py:130
  145.9 11.7 %copy-start.2 = (f32[8,4,2048]{2,1,0:T(4,128)}, f32[8,4,2048]{2,1,0:T(4,128)S(1)}, u32[]{:S(2)}) copy-start(f32[8,4,2048]{2,1,0:T(4,128)S(1)} %reshape.545) | copy-start | bytes 786436
  259.6 43.0 %all-to-all-start.3 = ((bf16[32,8,3,2048]{3,0,2,1:T(8,128)(2,1)}), bf16[32,8,3,2048]{3,0,2,1:T(8,128)(2,1)}, u32[]{:S(2)}, u32[]{:S(2)}) async-start(bf16[32,8,3,2048]{3,0,2,1:T(8,128)(2,1)} %copy.105), calls=%async_computation.3 | async-start | bytes 6291456 | tf_op jit(solution)/shard_map/all_to_all | solution.py:148
  302.6 41.8 %all-to-all-start.6 = ((s32[8,1,1]{2,1,0:T(1,128)}), s32[8,1,1]{2,1,0:T(1,128)S(1)}, u32[]{:S(2)}, u32[]{:S(2)}) async-start(s32[8,1,1]{2,1,0:T(1,128)} %copy.110), calls=%async_computation.6 | async-start | bytes 8192 | tf_op jit(solution)/shard_map/all_to_all | solution.py:120
  344.4 79.9 %all-to-all-start.4 = ((bf16[32,8,3,2048]{3,1,2,0:T(8,128)(2,1)}), bf16[32,8,3,2048]{3,1,2,0:T(8,128)(2,1)}, u32[]{:S(2)}, u32[]{:S(2)}) async-start(bf16[32,8,3,2048]{3,1,2,0:T(8,128)(2,1)} %copy.107), calls=%async_computation.4 | async-start | bytes 6291456 | tf_op jit(solution)/shard_map/all_to_all | solution.py:165
  424.3 54.5 %all-to-all-start.7 = ((bf16[8,1,16,128,128]{4,3,2,1,0:T(8,128)(2,1)}), bf16[8,1,16,128,128]{4,3,2,1,0:T(8,128)(2,1)}, u32[]{:S(2)}, u32[]{:S(2)}) async-start(bf16[8,1,16,128,128]{4,3,2,1,0:T(8,128)(2,1)} %bitcast.133), calls=%async_computation.7 | async-start | bytes 8388608 | tf_op jit(solution)/shard_map/all_to_all | solution.py:117
  434.4 48.8 %copy-start.24 = (f32[8,4,10]{2,1,0:T(4,128)S(1)}, f32[8,4,10]{2,1,0:T(4,128)}, u32[]{:S(2)}) copy-start(f32[8,4,10]{2,1,0:T(4,128)} %param.25) | copy-start | bytes 3844
  434.4 49.0 %copy-start.25 = (s32[320]{0:T(512)S(1)}, s32[320]{0:T(512)}, u32[]{:S(2)}) copy-start(s32[320]{0:T(512)} %fusion.52) | copy-start | bytes 3844
  478.8 42.9 %all-to-all-start.5 = ((bf16[32,8,3,2048]{3,0,2,1:T(8,128)(2,1)}), bf16[32,8,3,2048]{3,0,2,1:T(8,128)(2,1)}, u32[]{:S(2)}, u32[]{:S(2)}) async-start(bf16[32,8,3,2048]{3,0,2,1:T(8,128)(2,1)} %copy.108), calls=%async_computation.5 | async-start | bytes 6291456 | tf_op jit(solution)/shard_map/all_to_all | solution.py:164
  (12 other events, 59.7 us)
